TPU v7x, 128 devices: a whole 4x4x4 slice. The times are simulated.
128 devices in a mesh: ctx: 32 (over y, z, core), tp: 4 (over x).
Axes of the slice: x: 4, y: 4, z: 4, core: 2. Of those that a mesh axis runs over, the one named last changes fastest.
Arguments:
- tokens: bfloat16 [4096, 4096], P('ctx', 'tp'), may hold values from -6 to 6
- out_grad: bfloat16 [4096, 4096], P('ctx', 'tp'), may hold values from -4 to 4
- router_probs: bfloat16 [4096, 8], P('ctx'), may hold values from 0.049804688 to 0.5
- expert_ids: int32 [4096, 8], P('ctx'), may hold values from 0 to 63, all different within a row; in each aligned block of 128 rows (0 to 127, 128 to 255, ...) at most 24 rows name the same one
- w_gate: bfloat16 [64, 4096, 1536], P('ctx', None, 'tp'), may hold values from -0.09375 to 0.09375
- w_up: bfloat16 [64, 4096, 1536], P('ctx', None, 'tp'), may hold values from -0.09375 to 0.09375
- w_down: bfloat16 [64, 1536, 4096], P('ctx', 'tp'), may hold values from -0.15625 to 0.15625
Outputs:
- token_grad: bfloat16 [4096, 4096], P('ctx', 'tp')
- prob_grad: bfloat16 [4096, 8], P('ctx')
Inputs may be any that keep to these rules, and one draw needn't show every extreme that they name: `expert_ids`: each token names 8 different experts; among the 128 tokens of one index of ctx no expert is named by more than 24 tokens, a bound that some block reaches.
All inputs are finite; a program needn't handle non-finite values.
Results may differ from a plain program's by a relative error of at most 0.015.
Values may be sent and summed in bfloat16 or wider, within the bound.
A program may use at most 128 MiB of HBM per device.

v0:
```python
import jax
import jax.numpy as jnp
from jax import lax
from jax.sharding import PartitionSpec as P


def on_device(tokens, out_grad, router_probs, expert_ids, w_gate, w_up, w_down):
    groups = lax.axis_size("ctx")
    tok_rows, fanout = expert_ids.shape
    local_experts = w_gate.shape[0]
    experts_all = local_experts * groups
    capacity = 3 * tok_rows * fanout // (2 * experts_all)
    buffer_rows = experts_all * capacity
    flat_ids = expert_ids.reshape(tok_rows * fanout)
    expert_hot = (flat_ids[:, None] == jnp.arange(experts_all, dtype=jnp.int32)[None, :]).astype(
        jnp.int32
    )
    earlier = jnp.cumsum(expert_hot, axis=0) - expert_hot
    slot_index = jnp.sum(earlier * expert_hot, axis=1)
    target = flat_ids * capacity + slot_index
    row_hot = (target[:, None] == jnp.arange(buffer_rows, dtype=jnp.int32)[None, :]).astype(
        jnp.bfloat16
    )
    row_hot = row_hot.reshape(tok_rows, fanout, buffer_rows)
    selector = jnp.sum(row_hot, axis=1)
    prob_send = jnp.einsum("tkr,tk->r", row_hot, router_probs, preferred_element_type=jnp.float32)
    prob_send = prob_send.astype(jnp.bfloat16).reshape(groups, local_experts, capacity)

    def arrange(local_rows):
        placed = jnp.einsum("tr,td->rd", selector, local_rows, preferred_element_type=jnp.float32)
        return placed.astype(jnp.bfloat16).reshape(
            groups, local_experts, capacity, local_rows.shape[1]
        )

    full_tokens, full_grads = (
        lax.all_gather(tokens, "tp", axis=1, tiled=True),
        lax.all_gather(out_grad, "tp", axis=1, tiled=True),
    )
    x_rows, dy_rows, prob_rows = (
        lax.all_to_all(arrange(full_tokens), "ctx", split_axis=0, concat_axis=0, tiled=True),
        lax.all_to_all(arrange(full_grads), "ctx", split_axis=0, concat_axis=0, tiled=True),
        lax.all_to_all(prob_send, "ctx", split_axis=0, concat_axis=0, tiled=True),
    )
    gate_sum = jnp.einsum("secd,edf->secf", x_rows, w_gate, preferred_element_type=jnp.float32)
    up_sum = jnp.einsum("secd,edf->secf", x_rows, w_up, preferred_element_type=jnp.float32)
    down_back = jnp.einsum("secd,efd->secf", dy_rows, w_down, preferred_element_type=jnp.float32)
    sigmoid_gate = jax.nn.sigmoid(gate_sum)
    gated = gate_sum * sigmoid_gate
    hidden = gated * up_sum
    prob_part = jnp.sum(hidden * down_back, axis=3)
    prob_total = lax.psum(prob_part, "tp")
    hidden_grad = prob_rows.astype(jnp.float32)[..., None] * down_back
    gate_grad = (
        hidden_grad * up_sum * sigmoid_gate * (1.0 + gate_sum * (1.0 - sigmoid_gate))
    ).astype(jnp.bfloat16)
    up_grad = (hidden_grad * gated).astype(jnp.bfloat16)
    row_part = jnp.einsum("secf,edf->secd", gate_grad, w_gate, preferred_element_type=jnp.float32)
    row_part = row_part + jnp.einsum(
        "secf,edf->secd", up_grad, w_up, preferred_element_type=jnp.float32
    )
    row_grads = lax.psum_scatter(
        row_part.astype(jnp.bfloat16), "tp", scatter_dimension=3, tiled=True
    )
    back_rows, back_probs = (
        lax.all_to_all(row_grads, "ctx", split_axis=0, concat_axis=0, tiled=True),
        lax.all_to_all(
            prob_total.astype(jnp.bfloat16), "ctx", split_axis=0, concat_axis=0, tiled=True
        ),
    )
    token_grad = jnp.einsum(
        "tr,rd->td",
        selector,
        back_rows.reshape(buffer_rows, back_rows.shape[3]),
        preferred_element_type=jnp.float32,
    )
    prob_grad = back_probs.reshape(buffer_rows)[target].reshape(tok_rows, fanout)
    return (token_grad.astype(jnp.bfloat16), prob_grad)


def solution(mesh):
    return jax.shard_map(
        on_device,
        mesh=mesh,
        in_specs=(
            P("ctx", "tp"),
            P("ctx", "tp"),
            P("ctx", None),
            P("ctx", None),
            P("ctx", None, "tp"),
            P("ctx", None, "tp"),
            P("ctx", "tp", None),
        ),
        out_specs=(P("ctx", "tp"), P("ctx", None)),
        check_vma=False,
    )
```

profile of v0, /device:TPU:1, one launch (start us, length us, event | category | flops | bytes accessed | tf_op | source)
XLA Modules:
  0.0 695.2 jit_solution(9516662253684740646)
XLA Ops:
  7.2 0.7 all-gather.5.cloned.1.call-update
  7.9 0.8 copy.72
  8.7 0.1 eq.44
  8.8 0.1 eq.40
  8.9 0.8 copy.86
  9.7 18.0 %reduce-window.6 = s32[64,8,128]{2,1,0:T(8,128)S(1)} reduce-window(s32[64,8,128]{2,1,0:T(8,128)S(1)} %fusion.34, s32[]{:T(128)} %constant.4.clone.1), window={size=1x1x128 pad=0_0x0_0x127_0}, to_apply=%region_0.0 | reduce-window | flops 8323072 | bytes 524292 | tf_op jit(solution)/shard_map/reduce-window
  27.7 0.1 slice.10
  27.8 0.1 copy.75
  28.0 0.1 copy.76
  28.1 0.1 broadcast_add_fusion
  28.3 0.1 fusion.33
  28.3 0.1 reduce_sum.35
  28.4 0.6 broadcast_multiply_fusion
  29.1 1.2 fusion.30
  30.3 0.7 reshape.92
  31.0 9.6 %all-to-all-start = ((bf16[32,2,24]{2,1,0:T(2,128)(2,1)}), bf16[32,2,24]{2,1,0:T(2,128)(2,1)S(1)}, u32[]{:S(2)}, u32[]{:S(2)}) async-start(bf16[32,2,24]{2,1,0:T(2,128)(2,1)} %reshape.92), calls=%async_computation | async-start | bytes 32768 | tf_op jit(solution)/shard_map/all_to_all | solution.py:42
  40.6 3.1 fusion.15
  43.8 7.5 %convolution_convert_fusion = bf16[1536,4096]{1,0:T(8,128)(2,1)} fusion(bf16[128,1536]{1,0:T(8,128)(2,1)S(1)} %fusion.15, bf16[128,4096]{1,0:T(8,128)(2,1)} %all-gather.5.cloned.1.call-done), kind=kOutput, calls=%fused_computation.2 | convolution fusion | flops 1616904192 | bytes 14024704 | tf_op jit(solution)/shard_map/tr,td->rd/dot_general | solution.py:30
  51.3 7.4 %all-to-all-start.2 = ((bf16[32,2,24,4096]{3,2,1,0:T(8,128)(2,1)}), bf16[32,2,24,4096]{3,2,1,0:T(8,128)(2,1)}, u32[]{:S(2)}, u32[]{:S(2)}) async-start(bf16[32,2,24,4096]{3,2,1,0:T(8,128)(2,1)} %bitcast.101), calls=%async_computation.2 | async-start | bytes 25165824 | tf_op jit(solution)/shard_map/all_to_all | solution.py:40
  58.8 0.7 all-gather.3.cloned.1.call-update
  59.5 25.8 %all-gather.3.cloned.1.call-done = bf16[128,4096]{1,0:T(8,128)(2,1)} async-done(((bf16[128,1024]{1,0:T(8,128)(2,1)}), bf16[128,4096]{1,0:T(8,128)(2,1)}) %all-gather.3.cloned.1.call-update) | async-done | bytes 1048592 | tf_op jit(solution)/shard_map/all_gather | solution.py:37
  85.3 7.6 %convolution_convert_fusion.1 = bf16[1536,4096]{1,0:T(8,128)(2,1)} fusion(bf16[128,1536]{1,0:T(8,128)(2,1)S(1)} %fusion.15, bf16[128,4096]{1,0:T(8,128)(2,1)} %all-gather.3.cloned.1.call-done), kind=kOutput, calls=%fused_computation.3 | convolution fusion | flops 1616904192 | bytes 14024704 | tf_op jit(solution)/shard_map/tr,td->rd/dot_general | solution.py:30
  92.9 140.5 %all-to-all-done.2 = bf16[32,2,24,4096]{3,2,1,0:T(8,128)(2,1)} async-done(((bf16[32,2,24,4096]{3,2,1,0:T(8,128)(2,1)}), bf16[32,2,24,4096]{3,2,1,0:T(8,128)(2,1)}, u32[]{:S(2)}, u32[]{:S(2)}) %all-to-all-start.2) | async-done | bytes 12582944 | tf_op jit(solution)/shard_map/all_to_all | solution.py:40
  233.4 29.7 %all-to-all-start.1 = ((bf16[32,2,24,4096]{3,2,1,0:T(8,128)(2,1)}), bf16[32,2,24,4096]{3,2,1,0:T(8,128)(2,1)}, u32[]{:S(2)}, u32[]{:S(2)}) async-start(bf16[32,2,24,4096]{3,2,1,0:T(8,128)(2,1)} %bitcast.102), calls=%async_computation.1 | async-start | bytes 25165824 | tf_op jit(solution)/shard_map/all_to_all | solution.py:41
  263.1 0.2 reduce-scatter.2.cloned.1.call-start
  263.3 0.1 copy.77
  263.4 0.1 copy.78
  263.5 11.1 %fusion.3 = f32[2,32,24,384]{3,2,1,0:T(8,128)S(1)} fusion(bf16[32,2,24,4096]{3,2,1,0:T(8,128)(2,1)} %all-to-all-done.2, bf16[2,4096,384]{2,1,0:T(8,128)(2,1)} %param.11), kind=kOutput, calls=%fused_computation.7 | convolution fusion | flops 4831838208 | bytes 21233664 | tf_op jit(solution)/shard_map/secd,edf->secf/dot_general | solution.py:44
  274.5 163.2 %all-to-all-done.1 = bf16[32,2,24,4096]{3,2,1,0:T(8,128)(2,1)} async-done(((bf16[32,2,24,4096]{3,2,1,0:T(8,128)(2,1)}), bf16[32,2,24,4096]{3,2,1,0:T(8,128)(2,1)}, u32[]{:S(2)}, u32[]{:S(2)}) %all-to-all-start.1) | async-done | bytes 12582944 | tf_op jit(solution)/shard_map/all_to_all | solution.py:41
  437.7 11.1 %fusion.1 = f32[2,32,24,384]{3,2,1,0:T(8,128)S(1)} fusion(bf16[32,2,24,4096]{3,2,1,0:T(8,128)(2,1)} %all-to-all-done.1, bf16[2,384,4096]{2,1,0:T(8,128)(2,1)} %param.13), kind=kOutput, calls=%fused_computation.5 | convolution fusion | flops 4831838208 | bytes 21233664 | tf_op jit(solution)/shard_map/secd,efd->secf/dot_general | solution.py:46
  448.8 13.6 %fusion.25 = (f32[32,2,24]{2,0,1:T(8,128)S(1)}, f32[2,32,24,384]{3,2,1,0:T(8,128)}) fusion(f32[2,32,24,384]{3,2,1,0:T(8,128)S(1)} %fusion.1, f32[2,32,24,384]{3,2,1,0:T(8,128)S(1)} %fusion.3, bf16[2,4096,384]{2,1,0:T(8,128)(2,1)} %param.12, bf16[32,2,24,4096]{3,2,1,0:T(8,128)(2,1)} %all-to-all-done.2), kind=kOutput, calls=%fused_computation.35 | convolution fusion | flops 4835965440 | bytes 25958400 | tf_op jit(solution)/shard_map/secd,edf->secf/dot_general | solution.py:45
  462.5 16.0 %fusion.7 = f32[2,32,24,4096]{3,2,1,0:T(8,128)} fusion(bf16[2,4096,384]{2,1,0:T(8,128)(2,1)} %param.11, f32[2,32,24,384]{3,2,1,0:T(8,128)S(1)} %fusion.3, f32[2,32,24,384]{3,2,1,0:T(8,128)} %get-tuple-element.17, f32[2,32,24,384]{3,2,1,0:T(8,128)} %copy-done, f32[32,2,24]{2,0,1:T(8,128)S(1)} %copy.78), kind=kOutput, calls=%fused_computation.11 | convolution fusion | flops 4838326272 | bytes 38541312 | tf_op jit(solution)/shard_map/secf,edf->secd/dot_general | solution.py:57
  478.4 19.0 %fusion = bf16[32,2,24,4096]{3,2,0,1:T(8,128)(2,1)} fusion(f32[2,32,24,4096]{3,2,1,0:T(8,128)} %fusion.7, bf16[2,4096,384]{2,1,0:T(8,128)(2,1)} %param.12, f32[2,32,24,384]{3,2,1,0:T(8,128)} %copy-done, f32[32,2,24]{2,0,1:T(8,128)S(1)} %copy.78, f32[2,32,24,384]{3,2,1,0:T(8,128)S(1)} %fusion.3), kind=kOutput, calls=%fused_computation.4 | convolution fusion | flops 4848549888 | bytes 48764928 | tf_op jit(solution)/shard_map/secf,edf->secd/dot_general | solution.py:58
  497.4 0.1 copy.83
  497.5 13.3 %psum.7 = bf16[32,2,24]{0,2,1:T(8,128)(2,1)S(1)} all-reduce(f32[32,2,24]{0,2,1:T(8,128)S(1)} %copy.83), channel_id=1, replica_groups=mesh['ctx'=32,'tp'=4] {'tp'}, use_global_device_ids=true, to_apply=%region_6.7 | all-reduce | flops 1536 | bytes 9216 | tf_op jit(solution)/shard_map/psum | solution.py:51
  510.8 0.7 copy.84
  511.5 33.5 %all-to-all-start.4 = ((bf16[32,2,24]{2,1,0:T(2,128)(2,1)}), bf16[32,2,24]{2,1,0:T(2,128)(2,1)S(1)}, u32[]{:S(2)}, u32[]{:S(2)}) async-start(bf16[32,2,24]{2,1,0:T(2,128)(2,1)} %copy.84), calls=%async_computation.5 | async-start | bytes 32768 | tf_op jit(solution)/shard_map/all_to_all | solution.py:66
  545.0 90.3 %reduce-scatter.2.cloned.1.call-done = bf16[32,2,24,1024]{3,2,0,1:T(8,128)(2,1)} async-done(((bf16[32,2,24,4096]{3,2,0,1:T(8,128)(2,1)}), bf16[32,2,24,1024]{3,2,0,1:T(8,128)(2,1)}) %reduce-scatter.2.cloned.1.call-update) | async-done | bytes 3145744 | tf_op jit(solution)/shard_map/reduce_scatter | solution.py:61
  635.3 4.0 copy.82
  639.3 0.6 copy-done.1
  639.9 7.6 %all-to-all-start.3 = ((bf16[32,2,24,1024]{3,2,1,0:T(8,128)(2,1)}), bf16[32,2,24,1024]{3,2,1,0:T(8,128)(2,1)S(1)}, u32[]{:S(2)}, u32[]{:S(2)}) async-start(bf16[32,2,24,1024]{3,2,1,0:T(8,128)(2,1)} %copy.82), calls=%async_computation.4 | async-start | bytes 6291456 | tf_op jit(solution)/shard_map/all_to_all | solution.py:65
  647.6 0.9 mul.67
  648.5 0.8 reshape.96
  649.3 6.8 gather_fusion
  656.2 0.7 reshape.97
  656.9 1.4 copy.85
  658.3 29.1 %all-to-all-done.3 = bf16[32,2,24,1024]{3,2,1,0:T(8,128)(2,1)S(1)} async-done(((bf16[32,2,24,1024]{3,2,1,0:T(8,128)(2,1)}), bf16[32,2,24,1024]{3,2,1,0:T(8,128)(2,1)S(1)}, u32[]{:S(2)}, u32[]{:S(2)}) %all-to-all-start.3) | async-done | bytes 3145760 | tf_op jit(solution)/shard_map/all_to_all | solution.py:65
  687.3 1.3 convolution_convert_fusion.2
  (14 shorter events, 0.2 us)
Async XLA Ops:
  7.2 36.6 %all-gather.5.cloned.1.call-start = ((), (), s32[]{:S(2)}) async-start(), calls=%async_computation.7 | async-start | bytes 1310720 | tf_op jit(solution)/shard_map/all_gather | solution.py:36
  31.0 20.3 %all-to-all-start = ((bf16[32,2,24]{2,1,0:T(2,128)(2,1)}), bf16[32,2,24]{2,1,0:T(2,128)(2,1)S(1)}, u32[]{:S(2)}, u32[]{:S(2)}) async-start(bf16[32,2,24]{2,1,0:T(2,128)(2,1)} %reshape.92), calls=%async_computation | async-start | bytes 32768 | tf_op jit(solution)/shard_map/all_to_all | solution.py:42
  51.3 182.1 %all-to-all-start.2 = ((bf16[32,2,24,4096]{3,2,1,0:T(8,128)(2,1)}), bf16[32,2,24,4096]{3,2,1,0:T(8,128)(2,1)}, u32[]{:S(2)}, u32[]{:S(2)}) async-start(bf16[32,2,24,4096]{3,2,1,0:T(8,128)(2,1)} %bitcast.101), calls=%async_computation.2 | async-start | bytes 25165824 | tf_op jit(solution)/shard_map/all_to_all | solution.py:40
  58.7 26.6 %all-gather.3.cloned.1.call-start = ((), (), s32[]{:S(2)}) async-start(), calls=%async_computation.6 | async-start | bytes 1310720 | tf_op jit(solution)/shard_map/all_gather | solution.py:37
  233.4 204.3 %all-to-all-start.1 = ((bf16[32,2,24,4096]{3,2,1,0:T(8,128)(2,1)}), bf16[32,2,24,4096]{3,2,1,0:T(8,128)(2,1)}, u32[]{:S(2)}, u32[]{:S(2)}) async-start(bf16[32,2,24,4096]{3,2,1,0:T(8,128)(2,1)} %bitcast.102), calls=%async_computation.1 | async-start | bytes 25165824 | tf_op jit(solution)/shard_map/all_to_all | solution.py:41
  263.1 372.2 %reduce-scatter.2.cloned.1.call-start = ((), (), s32[]{:S(2)}) async-start(), calls=%async_computation.8 | async-start | bytes 15728640 | tf_op jit(solution)/shard_map/reduce_scatter | solution.py:61
  448.8 13.7 %copy-start = (f32[2,32,24,384]{3,2,1,0:T(8,128)}, f32[2,32,24,384]{3,2,1,0:T(8,128)S(1)}, u32[]{:S(2)}) copy-start(f32[2,32,24,384]{3,2,1,0:T(8,128)S(1)} %fusion.1) | copy-start | bytes 7077892
  511.5 127.8 %all-to-all-start.4 = ((bf16[32,2,24]{2,1,0:T(2,128)(2,1)}), bf16[32,2,24]{2,1,0:T(2,128)(2,1)S(1)}, u32[]{:S(2)}, u32[]{:S(2)}) async-start(bf16[32,2,24]{2,1,0:T(2,128)(2,1)} %copy.84), calls=%async_computation.5 | async-start | bytes 32768 | tf_op jit(solution)/shard_map/all_to_all | solution.py:66
  639.3 0.6 copy-start.1
  639.9 47.4 %all-to-all-start.3 = ((bf16[32,2,24,1024]{3,2,1,0:T(8,128)(2,1)}), bf16[32,2,24,1024]{3,2,1,0:T(8,128)(2,1)S(1)}, u32[]{:S(2)}, u32[]{:S(2)}) async-start(bf16[32,2,24,1024]{3,2,1,0:T(8,128)(2,1)} %copy.82), calls=%async_computation.4 | async-start | bytes 6291456 | tf_op jit(solution)/shard_map/all_to_all | solution.py:65
Sparse Core Ops, SparseCore 0:
  9.7 26.2 all-gather.4
  61.3 23.9 all-gather.2
  497.5 137.7 reduce-scatter.1
where the time goes:
time: 696 us; the launch traced here: 695 us
  waiting for transfers between devices  450 us (65%)
  matrix products  88.4 us (13%)
  starting transfers between devices  88.1 us (13%)
  other arithmetic  22 us (3%)
  local copies, waits for them, and re-layouts  19.1 us (3%)
  between operations  13.9 us (2%)
  blocking collectives  13.3 us (2%)
    all_to_all x1, waiting for transfers between devices, on_device(): lax.all_to_all(arrange(full_grads), 'ctx', split_axis=0, concat_axis=0, t...  163 us
    all_to_all x1, waiting for transfers between devices, on_device(): lax.all_to_all(arrange(full_tokens), 'ctx', split_axis=0, concat_axis=0,...  140 us
    reduce_scatter x1, waiting for transfers between devices, on_device(): lax.psum_scatter(row_part.astype(jnp.bfloat16), 'tp', scatter_dimension=3...  90.3 us
    all_to_all x1, starting transfers between devices, on_device(): lax.all_to_all(prob_total.astype(jnp.bfloat16), 'ctx', split_axis=0, conc...  33.5 us
    all_to_all x1, starting transfers between devices, on_device(): lax.all_to_all(arrange(full_grads), 'ctx', split_axis=0, concat_axis=0, t...  29.7 us
    all_to_all x1, waiting for transfers between devices, on_device(): lax.all_to_all(row_grads, 'ctx', split_axis=0, concat_axis=0, tiled=True)  29.1 us
    all_gather x1, waiting for transfers between devices, on_device(): lax.all_gather(out_grad, 'tp', axis=1, tiled=True)  25.8 us
    dot_general x1, matrix products, on_device(): jnp.einsum('secf,edf->secd', up_grad, w_up, preferred_element_type=jnp.fl...  19 us
  transfers between devices with their start and end apart: 8, of which 5 were waited for; matrix products, arithmetic and copies ran while one was open for 10% of the time, Pallas kernels for 0%

commit v1 on v0

--- a/solution.py
+++ b/solution.py
@@ -2,6 +2,19 @@
 import jax.numpy as jnp
 from jax import lax
 from jax.sharding import PartitionSpec as P
+
+
+def gather_around(value, axis, dim):
+    ways = lax.axis_size(axis)
+    up = [(d, (d + 1) % ways) for d in range(ways)]
+    down = [(d, (d - 1) % ways) for d in range(ways)]
+    earlier, later = ([value], [value])
+    for _ in range(ways // 2):
+        earlier.append(lax.ppermute(earlier[-1], axis, up))
+    for _ in range((ways - 1) // 2):
+        later.append(lax.ppermute(later[-1], axis, down))
+    line = jnp.concatenate([*earlier[::-1], *later[1:]], axis=dim)
+    return jnp.roll(line, (lax.axis_index(axis) - ways // 2) * value.shape[dim], axis=dim)
 
 
 def on_device(tokens, out_grad, router_probs, expert_ids, w_gate, w_up, w_down):
@@ -34,7 +47,7 @@
 
     full_tokens, full_grads = (
         lax.all_gather(tokens, "tp", axis=1, tiled=True),
-        lax.all_gather(out_grad, "tp", axis=1, tiled=True),
+        gather_around(out_grad, "tp", 1),
     )
     x_rows, dy_rows, prob_rows = (
         lax.all_to_all(arrange(full_tokens), "ctx", split_axis=0, concat_axis=0, tiled=True),

time: 696 us -> 697 us (level)
    all_gather x1 -> x0, waiting for transfers between devices: 25.8 us -> none  [on_device(): lax.all_gather(out_grad, 'tp', axis=1, tiled=True)]
    all_gather x1, waiting for transfers between devices: 0.02 us -> 25.7 us  [on_device(): lax.all_gather(tokens, 'tp', axis=1, tiled=True)]
    all_to_all x1, waiting for transfers between devices: 163 us -> 141 us  [on_device(): lax.all_to_all(arrange(full_grads), 'ctx', split_axis=0, concat_axis=0, t...]
    all_to_all x1, starting transfers between devices: 7.43 us -> 29.7 us  [on_device(): lax.all_to_all(arrange(full_tokens), 'ctx', split_axis=0, concat_axis=0,...]
    all_to_all x1, starting transfers between devices: 29.7 us -> 7.44 us  [on_device(): lax.all_to_all(arrange(full_grads), 'ctx', split_axis=0, concat_axis=0, t...]
    all_to_all x1, waiting for transfers between devices: 140 us -> 162 us  [on_device(): lax.all_to_all(arrange(full_tokens), 'ctx', split_axis=0, concat_axis=0,...]
  transfers between devices with their start and end apart: 8 -> 10, of which waited for: 5 -> 5; matrix products, arithmetic and copies ran while one was open for 10% -> 10% of each run, Pallas kernels for 0% -> 0%
where the time goes in v1:
time: 697 us
  waiting for transfers between devices  448 us (64%)
  starting transfers between devices  91.8 us (13%)
  matrix products  87.1 us (12%)
  other arithmetic  22 us (3%)
  local copies, waits for them, and re-layouts  19.3 us (3%)
  between operations  14.3 us (2%)
  blocking collectives  13.5 us (2%)
    all_to_all x1, waiting for transfers between devices, on_device(): lax.all_to_all(arrange(full_tokens), 'ctx', split_axis=0, concat_axis=0,...  162 us
    all_to_all x1, waiting for transfers between devices, on_device(): lax.all_to_all(arrange(full_grads), 'ctx', split_axis=0, concat_axis=0, t...  141 us
    reduce_scatter x1, waiting for transfers between devices, on_device(): lax.psum_scatter(row_part.astype(jnp.bfloat16), 'tp', scatter_dimension=3...  90 us
    all_to_all x1, starting transfers between devices, on_device(): lax.all_to_all(prob_total.astype(jnp.bfloat16), 'ctx', split_axis=0, conc...  33.5 us
    all_to_all x1, starting transfers between devices, on_device(): lax.all_to_all(arrange(full_tokens), 'ctx', split_axis=0, concat_axis=0,...  29.7 us
    all_to_all x1, waiting for transfers between devices, on_device(): lax.all_to_all(row_grads, 'ctx', split_axis=0, concat_axis=0, tiled=True)  29.1 us
    all_gather x1, waiting for transfers between devices, on_device(): lax.all_gather(tokens, 'tp', axis=1, tiled=True)  25.7 us
    dot_general x1, matrix products, on_device(): jnp.einsum('secf,edf->secd', up_grad, w_up, preferred_element_type=jnp.fl...  18.9 us
  transfers between devices with their start and end apart: 10, of which 5 were waited for; matrix products, arithmetic and copies ran while one was open for 10% of the time, Pallas kernels for 0%

profile of v1, /device:TPU:1, one launch (start us, length us, event | category | flops | bytes accessed | tf_op | source)
XLA Modules:
  0.0 696.6 jit_solution(18338977923162300880)
XLA Ops:
  7.2 2.1 collective-permute-start
  9.3 1.4 collective-permute-start.2
  10.6 0.8 copy.72
  11.4 0.1 eq.47
  11.5 0.1 eq.43
  11.6 18.0 %reduce-window.6 = s32[64,8,128]{2,1,0:T(8,128)S(1)} reduce-window(s32[64,8,128]{2,1,0:T(8,128)S(1)} %fusion.35, s32[]{:T(128)} %constant.36.clone.1), window={size=1x1x128 pad=0_0x0_0x127_0}, to_apply=%region_0.0 | reduce-window | flops 8323072 | bytes 524292 | tf_op jit(solution)/shard_map/reduce-window
  29.6 0.1 slice.10
  29.8 0.1 copy.75
  30.0 0.1 copy.76
  30.1 0.1 broadcast_add_fusion
  30.3 0.1 copy.86
  30.4 0.1 reduce_sum.35
  30.5 0.6 broadcast_multiply_fusion
  31.1 0.1 collective-permute-start.1
  31.3 1.2 fusion.30
  32.5 0.7 reshape.92
  33.2 9.7 %all-to-all-start = ((bf16[32,2,24]{2,1,0:T(2,128)(2,1)}), bf16[32,2,24]{2,1,0:T(2,128)(2,1)}, u32[]{:S(2)}, u32[]{:S(2)}) async-start(bf16[32,2,24]{2,1,0:T(2,128)(2,1)} %reshape.92), calls=%async_computation | async-start | bytes 32768 | tf_op jit(solution)/shard_map/all_to_all | solution.py:55
  42.9 3.1 fusion.15
  46.3 6.3 convolution_convert_fusion.1
  52.6 7.4 %all-to-all-start.1 = ((bf16[32,2,24,4096]{3,2,1,0:T(8,128)(2,1)}), bf16[32,2,24,4096]{3,2,1,0:T(8,128)(2,1)}, u32[]{:S(2)}, u32[]{:S(2)}) async-start(bf16[32,2,24,4096]{3,2,1,0:T(8,128)(2,1)} %bitcast.100), calls=%async_computation.1 | async-start | bytes 25165824 | tf_op jit(solution)/shard_map/all_to_all | solution.py:54
  60.1 0.7 all-gather.2.cloned.1.call-update
  60.8 25.7 %all-gather.2.cloned.1.call-done = bf16[128,4096]{1,0:T(8,128)(2,1)} async-done(((bf16[128,1024]{1,0:T(8,128)(2,1)}), bf16[128,4096]{1,0:T(8,128)(2,1)}) %all-gather.2.cloned.1.call-update) | async-done | bytes 1048592 | tf_op jit(solution)/shard_map/all_gather | solution.py:49
  86.5 7.6 %convolution_convert_fusion = bf16[1536,4096]{1,0:T(8,128)(2,1)} fusion(bf16[128,1536]{1,0:T(8,128)(2,1)S(1)} %fusion.15, bf16[128,4096]{1,0:T(8,128)(2,1)} %all-gather.2.cloned.1.call-done), kind=kOutput, calls=%fused_computation.2 | convolution fusion | flops 1616904192 | bytes 14024704 | tf_op jit(solution)/shard_map/tr,td->rd/dot_general | solution.py:43
  94.2 140.6 %all-to-all-done.1 = bf16[32,2,24,4096]{3,2,1,0:T(8,128)(2,1)} async-done(((bf16[32,2,24,4096]{3,2,1,0:T(8,128)(2,1)}), bf16[32,2,24,4096]{3,2,1,0:T(8,128)(2,1)}, u32[]{:S(2)}, u32[]{:S(2)}) %all-to-all-start.1) | async-done | bytes 12582944 | tf_op jit(solution)/shard_map/all_to_all | solution.py:54
  234.7 29.7 %all-to-all-start.2 = ((bf16[32,2,24,4096]{3,2,1,0:T(8,128)(2,1)}), bf16[32,2,24,4096]{3,2,1,0:T(8,128)(2,1)}, u32[]{:S(2)}, u32[]{:S(2)}) async-start(bf16[32,2,24,4096]{3,2,1,0:T(8,128)(2,1)} %bitcast.101), calls=%async_computation.2 | async-start | bytes 25165824 | tf_op jit(solution)/shard_map/all_to_all | solution.py:53
  264.4 0.2 reduce-scatter.2.cloned.1.call-start
  264.6 0.8 copy.77
  265.4 0.1 copy.78
  265.5 11.1 %fusion.1 = f32[2,32,24,384]{3,2,1,0:T(8,128)S(1)} fusion(bf16[32,2,24,4096]{3,2,1,0:T(8,128)(2,1)} %all-to-all-done.1, bf16[2,384,4096]{2,1,0:T(8,128)(2,1)} %param.13), kind=kOutput, calls=%fused_computation.5 | convolution fusion | flops 4831838208 | bytes 21233664 | tf_op jit(solution)/shard_map/secd,efd->secf/dot_general | solution.py:59
  276.6 162.4 %all-to-all-done.2 = bf16[32,2,24,4096]{3,2,1,0:T(8,128)(2,1)} async-done(((bf16[32,2,24,4096]{3,2,1,0:T(8,128)(2,1)}), bf16[32,2,24,4096]{3,2,1,0:T(8,128)(2,1)}, u32[]{:S(2)}, u32[]{:S(2)}) %all-to-all-start.2) | async-done | bytes 12582944 | tf_op jit(solution)/shard_map/all_to_all | solution.py:53
  439.0 11.1 %fusion.3 = f32[2,32,24,384]{3,2,1,0:T(8,128)S(1)} fusion(bf16[32,2,24,4096]{3,2,1,0:T(8,128)(2,1)} %all-to-all-done.2, bf16[2,4096,384]{2,1,0:T(8,128)(2,1)} %param.11), kind=kOutput, calls=%fused_computation.7 | convolution fusion | flops 4831838208 | bytes 21233664 | tf_op jit(solution)/shard_map/secd,edf->secf/dot_general | solution.py:57
  450.1 13.7 %fusion.25 = (f32[32,2,24]{2,0,1:T(8,128)S(1)}, f32[2,32,24,384]{3,2,1,0:T(8,128)}) fusion(f32[2,32,24,384]{3,2,1,0:T(8,128)S(1)} %fusion.1, f32[2,32,24,384]{3,2,1,0:T(8,128)S(1)} %fusion.3, bf16[2,4096,384]{2,1,0:T(8,128)(2,1)} %param.12, bf16[32,2,24,4096]{3,2,1,0:T(8,128)(2,1)} %all-to-all-done.2), kind=kOutput, calls=%fused_computation.35 | convolution fusion | flops 4835965440 | bytes 25958400 | tf_op jit(solution)/shard_map/secd,edf->secf/dot_general | solution.py:58
  463.8 15.8 %fusion.7 = f32[2,32,24,4096]{3,2,1,0:T(8,128)} fusion(bf16[2,4096,384]{2,1,0:T(8,128)(2,1)} %param.11, f32[2,32,24,384]{3,2,1,0:T(8,128)} %copy-done, f32[2,32,24,384]{3,2,1,0:T(8,128)} %get-tuple-element.17, f32[2,32,24,384]{3,2,1,0:T(8,128)S(1)} %fusion.1, f32[32,2,24]{2,0,1:T(8,128)S(1)} %copy.78), kind=kOutput, calls=%fused_computation.11 | convolution fusion | flops 4838326272 | bytes 38541312 | tf_op jit(solution)/shard_map/secf,edf->secd/dot_general | solution.py:70
  479.7 18.9 %fusion = bf16[32,2,24,4096]{3,2,0,1:T(8,128)(2,1)} fusion(f32[2,32,24,4096]{3,2,1,0:T(8,128)} %fusion.7, bf16[2,4096,384]{2,1,0:T(8,128)(2,1)} %param.12, f32[2,32,24,384]{3,2,1,0:T(8,128)S(1)} %fusion.1, f32[32,2,24]{2,0,1:T(8,128)S(1)} %copy.78, f32[2,32,24,384]{3,2,1,0:T(8,128)} %copy-done), kind=kOutput, calls=%fused_computation.4 | convolution fusion | flops 4848549888 | bytes 48764928 | tf_op jit(solution)/shard_map/secf,edf->secd/dot_general | solution.py:71
  498.7 13.5 %psum.7 = bf16[32,2,24]{0,2,1:T(8,128)(2,1)S(1)} all-reduce(f32[32,2,24]{0,2,1:T(8,128)S(1)} %copy.83), channel_id=1, replica_groups=mesh['ctx'=32,'tp'=4] {'tp'}, use_global_device_ids=true, to_apply=%region_6.7 | all-reduce | flops 1536 | bytes 9216 | tf_op jit(solution)/shard_map/psum | solution.py:64
  512.2 0.7 copy.84
  512.9 33.5 %all-to-all-start.4 = ((bf16[32,2,24]{2,1,0:T(2,128)(2,1)}), bf16[32,2,24]{2,1,0:T(2,128)(2,1)S(1)}, u32[]{:S(2)}, u32[]{:S(2)}) async-start(bf16[32,2,24]{2,1,0:T(2,128)(2,1)} %copy.84), calls=%async_computation.5 | async-start | bytes 32768 | tf_op jit(solution)/shard_map/all_to_all | solution.py:79
  546.4 90.0 %reduce-scatter.2.cloned.1.call-done = bf16[32,2,24,1024]{3,2,0,1:T(8,128)(2,1)} async-done(((bf16[32,2,24,4096]{3,2,0,1:T(8,128)(2,1)}), bf16[32,2,24,1024]{3,2,0,1:T(8,128)(2,1)}) %reduce-scatter.2.cloned.1.call-update) | async-done | bytes 3145744 | tf_op jit(solution)/shard_map/reduce_scatter | solution.py:74
  636.4 4.0 copy.82
  640.4 0.6 copy-done.2
  641.0 7.7 %all-to-all-start.3 = ((bf16[32,2,24,1024]{3,2,1,0:T(8,128)(2,1)}), bf16[32,2,24,1024]{3,2,1,0:T(8,128)(2,1)S(1)}, u32[]{:S(2)}, u32[]{:S(2)}) async-start(bf16[32,2,24,1024]{3,2,1,0:T(8,128)(2,1)} %copy.82), calls=%async_computation.4 | async-start | bytes 6291456 | tf_op jit(solution)/shard_map/all_to_all | solution.py:78
  648.7 0.9 mul.71
  649.6 0.8 reshape.96
  650.5 6.8 gather_fusion
  657.3 0.7 reshape.97
  658.0 1.4 copy.85
  659.4 29.1 %all-to-all-done.3 = bf16[32,2,24,1024]{3,2,1,0:T(8,128)(2,1)S(1)} async-done(((bf16[32,2,24,1024]{3,2,1,0:T(8,128)(2,1)}), bf16[32,2,24,1024]{3,2,1,0:T(8,128)(2,1)S(1)}, u32[]{:S(2)}, u32[]{:S(2)}) %all-to-all-start.3) | async-done | bytes 3145760 | tf_op jit(solution)/shard_map/all_to_all | solution.py:78
  688.4 1.3 convolution_convert_fusion.2
  (29 shorter events, 0.4 us)
Async XLA Ops:
  7.2 23.1 %copy-start.3 = (bf16[128,8]{0,1:T(8,128)(2,1)S(1)}, bf16[128,8]{0,1:T(8,128)(2,1)}, u32[]{:S(2)}) copy-start(bf16[128,8]{0,1:T(8,128)(2,1)} %param.9) | copy-start | bytes 6148
  7.2 24.0 %collective-permute-start = (bf16[128,1024]{1,0:T(8,128)(2,1)}, bf16[128,1024]{1,0:T(8,128)(2,1)S(1)}, u32[]{:S(2)}, u32[]{:S(2)}) collective-permute-start(bf16[128,1024]{1,0:T(8,128)(2,1)} %param.8), channel_id=1, source_target_pairs={{0,1},{1,2},{2,3},{3,0},{4,5},{5,6},{6,7},{7,4},{8,9},{9,10},{10,1... | collective-permute-start | bytes 786440 | tf_op jit(solution)/shard_map/ppermute | solution.py:13
  9.3 36.8 %collective-permute-start.2 = (bf16[128,1024]{1,0:T(8,128)(2,1)}, bf16[128,1024]{1,0:T(8,128)(2,1)S(1)}, u32[]{:S(2)}, u32[]{:S(2)}) collective-permute-start(bf16[128,1024]{1,0:T(8,128)(2,1)} %param.8), channel_id=1, source_target_pairs={{0,3},{1,0},{2,1},{3,2},{4,7},{5,4},{6,5},{7,6},{8,11},{9,8},{10,9... | collective-permute-start | bytes 786440 | tf_op jit(solution)/shard_map/ppermute | solution.py:15
  31.1 14.9 %collective-permute-start.1 = (bf16[128,1024]{1,0:T(8,128)(2,1)S(1)}, bf16[128,1024]{1,0:T(8,128)(2,1)S(1)}, u32[]{:S(2)}, u32[]{:S(2)}) collective-permute-start(bf16[128,1024]{1,0:T(8,128)(2,1)S(1)} %collective-permute-done), channel_id=1, source_target_pairs={{0,1},{1,2},{2,3},{3,0},{4,5},{5,6},{6,7},{7,4},{8,9},{9,10},{10,1... | collective-permute-start | bytes 786440 | tf_op jit(solution)/shard_map/ppermute | solution.py:13
  31.3 14.8 %copy-start.1 = (bf16[128,1024]{1,0:T(8,128)(2,1)S(1)}, bf16[128,1024]{1,0:T(8,128)(2,1)}, u32[]{:S(2)}) copy-start(bf16[128,1024]{1,0:T(8,128)(2,1)} %param.8) | copy-start | bytes 786436
  33.2 19.4 %all-to-all-start = ((bf16[32,2,24]{2,1,0:T(2,128)(2,1)}), bf16[32,2,24]{2,1,0:T(2,128)(2,1)}, u32[]{:S(2)}, u32[]{:S(2)}) async-start(bf16[32,2,24]{2,1,0:T(2,128)(2,1)} %reshape.92), calls=%async_computation | async-start | bytes 32768 | tf_op jit(solution)/shard_map/all_to_all | solution.py:55
  52.6 182.1 %all-to-all-start.1 = ((bf16[32,2,24,4096]{3,2,1,0:T(8,128)(2,1)}), bf16[32,2,24,4096]{3,2,1,0:T(8,128)(2,1)}, u32[]{:S(2)}, u32[]{:S(2)}) async-start(bf16[32,2,24,4096]{3,2,1,0:T(8,128)(2,1)} %bitcast.100), calls=%async_computation.1 | async-start | bytes 25165824 | tf_op jit(solution)/shard_map/all_to_all | solution.py:54
  60.0 26.5 %all-gather.2.cloned.1.call-start = ((), (), s32[]{:S(2)}) async-start(), calls=%async_computation.6 | async-start | bytes 1310720 | tf_op jit(solution)/shard_map/all_gather | solution.py:49
  234.7 204.3 %all-to-all-start.2 = ((bf16[32,2,24,4096]{3,2,1,0:T(8,128)(2,1)}), bf16[32,2,24,4096]{3,2,1,0:T(8,128)(2,1)}, u32[]{:S(2)}, u32[]{:S(2)}) async-start(bf16[32,2,24,4096]{3,2,1,0:T(8,128)(2,1)} %bitcast.101), calls=%async_computation.2 | async-start | bytes 25165824 | tf_op jit(solution)/shard_map/all_to_all | solution.py:53
  264.4 372.0 %reduce-scatter.2.cloned.1.call-start = ((), (), s32[]{:S(2)}) async-start(), calls=%async_computation.7 | async-start | bytes 15728640 | tf_op jit(solution)/shard_map/reduce_scatter | solution.py:74
  450.1 13.8 %copy-start = (f32[2,32,24,384]{3,2,1,0:T(8,128)}, f32[2,32,24,384]{3,2,1,0:T(8,128)S(1)}, u32[]{:S(2)}) copy-start(f32[2,32,24,384]{3,2,1,0:T(8,128)S(1)} %fusion.3) | copy-start | bytes 7077892
  512.9 127.5 %all-to-all-start.4 = ((bf16[32,2,24]{2,1,0:T(2,128)(2,1)}), bf16[32,2,24]{2,1,0:T(2,128)(2,1)S(1)}, u32[]{:S(2)}, u32[]{:S(2)}) async-start(bf16[32,2,24]{2,1,0:T(2,128)(2,1)} %copy.84), calls=%async_computation.5 | async-start | bytes 32768 | tf_op jit(solution)/shard_map/all_to_all | solution.py:79
  640.4 0.6 copy-start.2
  641.0 47.4 %all-to-all-start.3 = ((bf16[32,2,24,1024]{3,2,1,0:T(8,128)(2,1)}), bf16[32,2,24,1024]{3,2,1,0:T(8,128)(2,1)S(1)}, u32[]{:S(2)}, u32[]{:S(2)}) async-start(bf16[32,2,24,1024]{3,2,1,0:T(8,128)(2,1)} %copy.82), calls=%async_computation.4 | async-start | bytes 6291456 | tf_op jit(solution)/shard_map/all_to_all | solution.py:78
Sparse Core Ops, SparseCore 0:
  62.5 23.9 all-gather.1
  498.7 137.6 reduce-scatter.1
